TPU v7x, 256 devices: a whole 4x4x8 slice. The times are simulated.
256 devices in a mesh: pole: 4 (over y), row: 8 (over z_lo, x), col: 8 (over z_hi, core).
Axes of the slice: x: 4, y: 4, z: 8 (z_hi: 4, z_lo: 2; z = z_hi * 2 + z_lo), core: 2. Of those that a mesh axis runs over, the one named last changes fastest.
Arguments:
- found_inverse: bfloat16 [4, 2, 8192, 8, 8, 128], P('pole', None, 'row', None, 'col'), may hold values from -0.125 to 0.125
- l_panel: bfloat16 [4, 2, 8192, 512], P('pole', None, ('row', 'col')), may hold values from -1.5 to 1.5
- block_pattern: int32 [64, 4], P(('row', 'col')), may hold values 0 or 1
- sup_widths: int32 [4], replicated, may hold values from 1 to 128, 320 in all
- diag_inverse: bfloat16 [4, 2, 512, 128], P('pole'), may hold values from -6 to 6
- pole_weights: float32 [4, 2], P('pole'), may hold values from -4 to 4
Outputs:
- density: float32 [512, 8192], P('col', 'row')
- diagonal: float32 [512, 128], replicated
Inputs may be any that keep to these rules, and one draw needn't show every extreme that they name: `sup_widths`: one supernode has exactly 128 columns.
All inputs are finite; a program needn't handle non-finite values. No bound on the sum of `block_pattern` on one device may be relied on, other than what follows from the above.
Results may differ from a plain program's by a relative error of at most 0.0003.
Values may be sent and summed in bfloat16 or wider, within the bound.
A program may use at most 128 MiB of HBM per device.

v0:
```python
import jax
import jax.numpy as jnp
from jax import lax
from jax.sharding import PartitionSpec as P


def contract(left, right):
    return jnp.einsum("jk,ij->ki", left, right, preferred_element_type=jnp.float32)


def pair_product(left, right):
    return jnp.einsum("ika,kbi->kab", left, right, precision=lax.Precision.HIGHEST)


def per_device(found_inverse, l_panel, block_pattern, sup_widths, diag_inverse, pole_weights):
    slot_width = diag_inverse.shape[-1]
    total_cols = l_panel.shape[-1]
    supernodes = total_cols // slot_width
    row_count = lax.axis_size("row")
    row_index = lax.axis_index("row")
    col_index = lax.axis_index("col")
    columns = jnp.arange(total_cols, dtype=jnp.int32)
    column_ok = columns % slot_width < jnp.repeat(sup_widths, slot_width)
    block_ok = jnp.repeat(block_pattern[0], slot_width) == 1
    masked = jnp.where(
        (column_ok & block_ok)[None, None, :], l_panel[0], jnp.zeros((), jnp.bfloat16)
    )
    column_rows = lax.all_gather(masked, "row", axis=1, tiled=True)
    own_rows = lax.all_gather(masked, "col", axis=1, tiled=True)
    local_rows = found_inverse.shape[2]
    inverse = found_inverse[0].reshape(2, local_rows, row_count * slot_width)
    part_real = contract(column_rows[1], inverse[1]) - contract(column_rows[0], inverse[0])
    part_imag = -(contract(column_rows[1], inverse[0]) + contract(column_rows[0], inverse[1]))
    w_real = pole_weights[0, 0]
    w_imag = pole_weights[0, 1]
    weighted = w_real * part_real - w_imag * part_imag
    part = lax.psum_scatter(weighted, "col", scatter_dimension=0, tiled=True)
    density = lax.psum(part, "pole")
    lifted = own_rows.astype(jnp.float32).reshape(2, local_rows, supernodes, slot_width)
    upper_real = part_real.reshape(supernodes, slot_width, local_rows)
    upper_imag = part_imag.reshape(supernodes, slot_width, local_rows)
    t_real = pair_product(lifted[0], upper_real) - pair_product(lifted[1], upper_imag)
    t_imag = pair_product(lifted[0], upper_imag) + pair_product(lifted[1], upper_real)
    lead_flag = ((row_index == 0) & (col_index == 0)).astype(jnp.float32)
    d_real = diag_inverse[0, 0].astype(jnp.float32).reshape(supernodes, slot_width, slot_width)
    d_imag = diag_inverse[0, 1].astype(jnp.float32).reshape(supernodes, slot_width, slot_width)
    local_term = lead_flag * (w_real * d_real - w_imag * d_imag) - (
        w_real * t_real - w_imag * t_imag
    )
    diagonal = lax.psum(local_term.reshape(total_cols, slot_width), ("pole", "row", "col"))
    return (density, diagonal)


def solution(mesh):
    in_specs = (
        P("pole", None, "row", None, "col", None),
        P("pole", None, ("row", "col"), None),
        P(("row", "col"), None),
        P(),
        P("pole", None, None, None),
        P("pole", None),
    )
    out_specs = (P("col", "row"), P())
    return jax.shard_map(
        per_device, mesh=mesh, in_specs=in_specs, out_specs=out_specs, check_vma=False
    )
```

profile of v0, /device:TPU:2, one launch (start us, length us, event | category | flops | bytes accessed | tf_op | source)
XLA Modules:
  0.0 457.6 jit_solution(11535285280863356408)
XLA Ops:
  7.2 0.0 all-gather.3.cloned.1.call-start
  7.2 0.7 compare_bitcast_fusion
  7.9 0.7 fusion.25
  8.6 1.7 bitcast_select_fusion
  10.3 0.0 all-gather.3.cloned.1.call-update
  10.3 0.0 all-gather.5.cloned.1.call-start
  10.3 0.7 all-gather.5.cloned.1.call-update
  11.1 0.0 reduce-scatter.2.cloned.1.call-start
  11.1 1.4 fusion.28
  12.5 3.8 fusion.26
  16.3 38.6 %all-gather.3.cloned.1.call-done = bf16[2,1024,512]{2,1,0:T(8,128)(2,1)} async-done(((bf16[2,128,512]{2,1,0:T(8,128)(2,1)}), bf16[2,1024,512]{2,1,0:T(8,128)(2,1)}) %all-gather.3.cloned.1.call-update) | async-done | bytes 2097168 | tf_op jit(solution)/shard_map/all_gather | solution.py:28
  54.9 0.0 copy-start.3
  54.9 2.7 fusion.2
  57.6 0.0 copy-done.3
  57.6 0.0 copy-start.2
  57.6 1.3 fusion
  58.9 0.3 copy-done.2
  59.2 1.3 fusion.12
  60.5 4.6 %multiply_subtract_fusion = (f32[512,1024]{1,0:T(8,128)}, f32[512,1024]{1,0:T(8,128)}) fusion(f32[512,1024]{1,0:T(8,128)S(1)} %fusion.12, f32[]{:T(128)} %bitcast.7, f32[]{:T(128)} %bitcast, f32[512,1024]{1,0:T(8,128)S(1)} %fusion, bf16[128,8,8,128]{3,2,1,0:T(8,128)(2,1)S(1)} %bitcast.67, bf16[2,1024,512]{2,1,0:T(8,128)(2,1)S(1)} %copy-done.3), kind=kOutput, calls=%fused_computation.8 | convolution fusion | flops 1076363264 | bytes 11534344 | tf_op jit(solution)/shard_map/jk,ij->ki/dot_general | solution.py:8
  65.1 0.0 copy-start.4
  65.1 0.0 reduce-scatter.2.cloned.1.call-update
  65.1 0.0 all-reduce.5.cloned.1.call-start
  65.2 0.9 copy-done.4
  66.1 1.3 subtract_multiply_fusion
  67.4 27.9 %all-gather.5.cloned.1.call-done = bf16[2,1024,512]{2,1,0:T(8,128)(2,1)} async-done(((bf16[2,128,512]{2,1,0:T(8,128)(2,1)}), bf16[2,1024,512]{2,1,0:T(8,128)(2,1)}) %all-gather.5.cloned.1.call-update) | async-done | bytes 2097168 | tf_op jit(solution)/shard_map/all_gather | solution.py:29
  95.3 2.7 fusion.27
  97.9 1.3 copy.8
  99.3 1.5 copy.9
  100.8 0.0 copy-start
  100.8 0.0 copy-start.1
  100.8 2.5 fusion.29
  103.3 0.0 copy-done
  103.3 0.0 copy-done.1
  103.3 1.2 fusion.30
  104.5 1.9 fusion.20
  106.4 2.5 fusion.19
  108.9 0.0 all-reduce.5.cloned.1.call-update
  108.9 0.0 all-reduce.3.cloned.1.call-start
  109.0 31.0 %reduce-scatter.2.cloned.1.call-done = f32[64,1024]{1,0:T(8,128)} async-done(((f32[512,1024]{1,0:T(8,128)}), f32[64,1024]{1,0:T(8,128)}) %reduce-scatter.2.cloned.1.call-update) | async-done | bytes 262160 | tf_op jit(solution)/shard_map/reduce_scatter | solution.py:37
  140.0 0.0 all-reduce.3.cloned.1.call-update
  140.1 259.7 %all-reduce.5.cloned.1.call-done = f32[512,128]{1,0:T(8,128)} async-done(((f32[512,128]{1,0:T(8,128)}), f32[512,128]{1,0:T(8,128)}) %all-reduce.5.cloned.1.call-update) | async-done | bytes 262160 | tf_op jit(solution)/shard_map/psum | solution.py:50
  399.8 48.0 %all-reduce.3.cloned.1.call-done = f32[64,1024]{1,0:T(8,128)} async-done(((f32[64,1024]{1,0:T(8,128)}), f32[64,1024]{1,0:T(8,128)}) %all-reduce.3.cloned.1.call-update) | async-done | bytes 262160 | tf_op jit(solution)/shard_map/psum | solution.py:38
  447.8 1.7 copy.36
  449.4 1.7 copy.37
Async XLA Ops:
  7.2 47.7 %all-gather.3.cloned.1.call-start = ((), (), s32[]{:S(2)}) async-start(), calls=%async_computation.1 | async-start | bytes 2359296 | tf_op jit(solution)/shard_map/all_gather | solution.py:28
  10.3 85.0 %all-gather.5.cloned.1.call-start = ((), (), s32[]{:S(2)}) async-start(), calls=%async_computation.4 | async-start | bytes 2359296 | tf_op jit(solution)/shard_map/all_gather | solution.py:29
  11.1 129.0 %reduce-scatter.2.cloned.1.call-start = ((), (), s32[]{:S(2)}) async-start(), calls=%async_computation.2 | async-start | bytes 2359296 | tf_op jit(solution)/shard_map/reduce_scatter | solution.py:37
  54.9 2.7 copy-start.3
  57.6 1.6 copy-start.2
  65.1 0.9 copy-start.4
  65.1 334.7 %all-reduce.5.cloned.1.call-start = ((), (), s32[]{:S(2)}) async-start(), calls=%async_computation.5 | async-start | bytes 524288 | tf_op jit(solution)/shard_map/psum | solution.py:50
  100.8 2.6 copy-start
  100.8 2.6 copy-start.1
  108.9 338.8 %all-reduce.3.cloned.1.call-start = ((), (), s32[]{:S(2)}) async-start(), calls=%async_computation.3 | async-start | bytes 524288 | tf_op jit(solution)/shard_map/psum | solution.py:38
Sparse Core Ops, SparseCore 0:
  10.4 44.4 all-gather.2
  57.3 37.9 all-gather.4
  97.8 42.1 reduce-scatter.1
  145.9 253.8 all-reduce.4
  402.0 45.7 all-reduce.2
where the time goes:
time: 458 us
  waiting for transfers between devices  406 us (89%)
  matrix products  18 us (4%)
  local copies, waits for them, and re-layouts  15.2 us (3%)
  between operations  13.9 us (3%)
    psum x1, waiting for transfers between devices, per_device(): lax.psum(local_term.reshape(total_cols, slot_width), ('pole', 'row', 'col'))  260 us
    psum x1, waiting for transfers between devices, per_device(): density = lax.psum(part, 'pole')  48 us
    all_gather x1, waiting for transfers between devices, per_device(): column_rows = lax.all_gather(masked, 'row', axis=1, tiled=True)  38.6 us
    reduce_scatter x1, waiting for transfers between devices, per_device(): part = lax.psum_scatter(weighted, 'col', scatter_dimension=0, tiled=True)  31 us
    all_gather x1, waiting for transfers between devices, per_device(): own_rows = lax.all_gather(masked, 'col', axis=1, tiled=True)  27.9 us
    dot_general x4, matrix products, contract(): jnp.einsum('jk,ij->ki', left, right, preferred_element_type=jnp.float32)  9.92 us
  transfers between devices with their start and end apart: 5, of which 5 were waited for; matrix products, arithmetic and copies ran while one was open for 7% of the time, Pallas kernels for 0%

commit v1 on v0

--- a/solution.py
+++ b/solution.py
@@ -35,7 +35,9 @@
     w_imag = pole_weights[0, 1]
     weighted = w_real * part_real - w_imag * part_imag
     part = lax.psum_scatter(weighted, "col", scatter_dimension=0, tiled=True)
-    density = lax.psum(part, "pole")
+    density = part
+    for hop in (1, 2):
+        density = density + lax.ppermute(density, "pole", [(dev, dev ^ hop) for dev in range(4)])
     lifted = own_rows.astype(jnp.float32).reshape(2, local_rows, supernodes, slot_width)
     upper_real = part_real.reshape(supernodes, slot_width, local_rows)
     upper_imag = part_imag.reshape(supernodes, slot_width, local_rows)

time: 458 us -> 414 us (0.904)
  waiting for transfers between devices: 406 us -> 353 us
    psum x1 -> x0, waiting for transfers between devices: 48 us -> none  [per_device(): density = lax.psum(part, 'pole')]
    psum x1, waiting for transfers between devices: 260 us -> 248 us  [per_device(): lax.psum(local_term.reshape(total_cols, slot_width), ('pole', 'row', 'col'))]
  transfers between devices with their start and end apart: 5 -> 6, of which waited for: 5 -> 6; matrix products, arithmetic and copies ran while one was open for 7% -> 9% of each run, Pallas kernels for 0% -> 0%
where the time goes in v1:
time: 414 us; the launch traced here: 413 us
  waiting for transfers between devices  353 us (85%)
  matrix products  20.8 us (5%)
  between operations  13.9 us (3%)
  local copies, waits for them, and re-layouts  13.5 us (3%)
  other arithmetic  6.84 us (2%)
  starting transfers between devices  4.66 us (1%)
    psum x1, waiting for transfers between devices, per_device(): lax.psum(local_term.reshape(total_cols, slot_width), ('pole', 'row', 'col'))  248 us
    all_gather x1, waiting for transfers between devices, per_device(): column_rows = lax.all_gather(masked, 'row', axis=1, tiled=True)  38.5 us
    reduce_scatter x1, waiting for transfers between devices, per_device(): part = lax.psum_scatter(weighted, 'col', scatter_dimension=0, tiled=True)  34.5 us
    all_gather x1, waiting for transfers between devices, per_device(): own_rows = lax.all_gather(masked, 'col', axis=1, tiled=True)  27 us
    dot_general x4, matrix products, pair_product(): jnp.einsum('ika,kbi->kab', left, right, precision=lax.Precision.HIGHEST)  10.8 us
    dot_general x4, matrix products, contract(): jnp.einsum('jk,ij->ki', left, right, preferred_element_type=jnp.float32)  10 us
  transfers between devices with their start and end apart: 6, of which 6 were waited for; matrix products, arithmetic and copies ran while one was open for 9% of the time, Pallas kernels for 0%

profile of v1, /device:TPU:2, one launch (start us, length us, event | category | flops | bytes accessed | tf_op | source)
XLA Modules:
  0.0 413.1 jit_solution(10683828812928990843)
XLA Ops:
  7.2 0.0 all-gather.3.cloned.1.call-start
  7.2 0.7 compare_bitcast_fusion
  7.9 0.7 fusion.25
  8.6 1.7 bitcast_select_fusion
  10.3 0.0 all-gather.3.cloned.1.call-update
  10.3 0.0 all-gather.5.cloned.1.call-start
  10.3 0.7 all-gather.5.cloned.1.call-update
  11.1 0.0 reduce-scatter.2.cloned.1.call-start
  11.1 1.4 fusion.28
  12.5 3.9 fusion.26
  16.3 38.5 %all-gather.3.cloned.1.call-done = bf16[2,1024,512]{2,1,0:T(8,128)(2,1)} async-done(((bf16[2,128,512]{2,1,0:T(8,128)(2,1)}), bf16[2,1024,512]{2,1,0:T(8,128)(2,1)}) %all-gather.3.cloned.1.call-update) | async-done | bytes 2097168 | tf_op jit(solution)/shard_map/all_gather | solution.py:28
  54.9 0.0 copy-start.4
  54.9 2.7 fusion.2
  57.6 0.0 copy-done.4
  57.6 0.0 copy-start.1
  57.6 1.3 fusion
  58.9 0.3 copy-done.1
  59.2 1.3 fusion.12
  60.5 4.8 %multiply_subtract_fusion = (f32[512,1024]{1,0:T(8,128)}, f32[512,1024]{1,0:T(8,128)}) fusion(f32[512,1024]{1,0:T(8,128)S(1)} %fusion.12, f32[]{:T(128)} %bitcast.7, f32[]{:T(128)} %bitcast, f32[512,1024]{1,0:T(8,128)S(1)} %fusion, bf16[128,8,8,128]{3,2,1,0:T(8,128)(2,1)S(1)} %bitcast.67, bf16[2,1024,512]{2,1,0:T(8,128)(2,1)S(1)} %copy-done.4), kind=kOutput, calls=%fused_computation.8 | convolution fusion | flops 1076363264 | bytes 11534344 | tf_op jit(solution)/shard_map/jk,ij->ki/dot_general | solution.py:8
  65.2 0.0 copy-start.6
  65.2 0.0 reduce-scatter.2.cloned.1.call-update
  65.3 0.0 all-reduce.2.cloned.1.call-start
  65.3 0.9 copy-done.6
  66.2 2.1 subtract_multiply_fusion
  68.2 27.0 %all-gather.5.cloned.1.call-done = bf16[2,1024,512]{2,1,0:T(8,128)(2,1)} async-done(((bf16[2,128,512]{2,1,0:T(8,128)(2,1)}), bf16[2,1024,512]{2,1,0:T(8,128)(2,1)}) %all-gather.5.cloned.1.call-update) | async-done | bytes 2097168 | tf_op jit(solution)/shard_map/all_gather | solution.py:29
  95.3 2.7 fusion.27
  97.9 1.3 copy.8
  99.2 1.5 copy.9
  100.7 0.0 copy-start
  100.7 2.5 fusion.29
  103.3 0.0 copy-done
  103.3 2.5 fusion.20
  105.8 34.5 %reduce-scatter.2.cloned.1.call-done = f32[64,1024]{1,0:T(8,128)} async-done(((f32[512,1024]{1,0:T(8,128)}), f32[64,1024]{1,0:T(8,128)}) %reduce-scatter.2.cloned.1.call-update) | async-done | bytes 262160 | tf_op jit(solution)/shard_map/reduce_scatter | solution.py:37
  140.3 0.0 copy-start.5
  140.3 0.0 copy-start.2
  140.3 1.3 collective-permute-start
  141.6 3.1 fusion.30
  144.7 2.2 collective-permute-done
  146.9 0.0 copy-done.5
  146.9 3.2 collective-permute-start.1
  150.1 0.0 copy-done.2
  150.1 0.0 copy-done.3
  150.1 2.6 fusion.19
  152.7 0.0 all-reduce.2.cloned.1.call-update
  152.7 2.3 collective-permute-done.1
  155.0 1.7 add.29
  156.7 248.2 %all-reduce.2.cloned.1.call-done = f32[512,128]{1,0:T(8,128)} async-done(((f32[512,128]{1,0:T(8,128)}), f32[512,128]{1,0:T(8,128)}) %all-reduce.2.cloned.1.call-update) | async-done | bytes 262160 | tf_op jit(solution)/shard_map/psum | solution.py:52
  404.9 1.7 copy.35
  (2 shorter events, 0.0 us)
Async XLA Ops:
  7.2 47.7 %all-gather.3.cloned.1.call-start = ((), (), s32[]{:S(2)}) async-start(), calls=%async_computation.1 | async-start | bytes 2359296 | tf_op jit(solution)/shard_map/all_gather | solution.py:28
  10.3 85.0 %all-gather.5.cloned.1.call-start = ((), (), s32[]{:S(2)}) async-start(), calls=%async_computation.3 | async-start | bytes 2359296 | tf_op jit(solution)/shard_map/all_gather | solution.py:29
  11.1 129.3 %reduce-scatter.2.cloned.1.call-start = ((), (), s32[]{:S(2)}) async-start(), calls=%async_computation.2 | async-start | bytes 2359296 | tf_op jit(solution)/shard_map/reduce_scatter | solution.py:37
  54.9 2.7 copy-start.4
  57.6 1.6 copy-start.1
  65.2 0.9 copy-start.6
  65.3 339.7 %all-reduce.2.cloned.1.call-start = ((), (), s32[]{:S(2)}) async-start(), calls=%async_computation.4 | async-start | bytes 524288 | tf_op jit(solution)/shard_map/psum | solution.py:52
  100.7 2.6 copy-start
  140.3 6.6 %copy-start.5 = (f32[64,1024]{1,0:T(8,128)S(1)}, f32[64,1024]{1,0:T(8,128)}, u32[]{:S(2)}) copy-start(f32[64,1024]{1,0:T(8,128)} %reduce-scatter.2.cloned.1.call-done) | copy-start | bytes 786436
  140.3 9.8 %copy-start.2 = (f32[1,1,512,128]{3,2,1,0:T(8,128)S(1)}, f32[1,1,512,128]{3,2,1,0:T(8,128)}, u32[]{:S(2)}) copy-start(f32[1,1,512,128]{3,2,1,0:T(8,128)} %subtract_multiply_fusion) | copy-start | bytes 786436
  140.3 9.8 %copy-start.3 = (f32[4,128,128]{2,1,0:T(8,128)S(1)}, f32[4,128,128]{2,1,0:T(8,128)}, u32[]{:S(2)}) copy-start(f32[4,128,128]{2,1,0:T(8,128)} %fusion.20) | copy-start | bytes 786436
  140.3 6.6 %collective-permute-start = (f32[64,1024]{1,0:T(8,128)}, f32[64,1024]{1,0:T(8,128)S(1)}, u32[]{:S(2)}, u32[]{:S(2)}) collective-permute-start(f32[64,1024]{1,0:T(8,128)} %reduce-scatter.2.cloned.1.call-done), channel_id=1, source_target_pairs={{0,64},{64,0},{128,192},{192,128},{1,65},{65,1},{129,193},{193,129... | collective-permute-start | bytes 786440 | tf_op jit(solution)/shard_map/ppermute | solution.py:40
  146.9 8.1 %collective-permute-start.1 = (f32[64,1024]{1,0:T(8,128)S(1)}, f32[64,1024]{1,0:T(8,128)}, u32[]{:S(2)}, u32[]{:S(2)}) collective-permute-start(f32[64,1024]{1,0:T(8,128)S(1)} %add.28), channel_id=1, source_target_pairs={{0,128},{64,192},{128,0},{192,64},{1,129},{65,193},{129,1},{193,65... | collective-permute-start | bytes 786440 | tf_op jit(solution)/shard_map/ppermute | solution.py:40
Sparse Core Ops, SparseCore 0:
  10.4 44.4 all-gather.2
  57.3 37.9 all-gather.4
  97.8 42.4 reduce-scatter.1
  152.8 252.0 all-reduce.1
